TPU v7x, 32 devices: a whole 2x2x4 slice. The times are simulated.
32 devices in a mesh: dp: 2 (over core), expert: 16 (over z, y, x).
Axes of the slice: x: 2, y: 2, z: 4, core: 2. Of those that a mesh axis runs over, the one named last changes fastest.
Arguments:
- tokens: bfloat16 [2048, 2048], P('expert'), may hold values from -6 to 6
- out_grad: bfloat16 [2048, 2048], P('expert'), may hold values from -6 to 6
- route_ids: int32 [2048, 8], P('expert'), may hold values from 0 to 15, all different within a row; in each aligned block of 128 rows (0 to 127, 128 to 255, ...) at most 72 rows name the same one
- route_probs: float32 [2048, 8], P('expert'), may hold values from 0.05 to 1
- gate_store: bfloat16 [16, 2048, 768], P(None, 'expert', 'dp'), may hold values from -0.125 to 0.125
- up_store: bfloat16 [16, 2048, 768], P(None, 'expert', 'dp'), may hold values from -0.125 to 0.125
- down_store: bfloat16 [16, 2048, 768], P(None, 'expert', 'dp'), may hold values from -0.21875 to 0.21875
Outputs:
- grad_gate: bfloat16 [16, 2048, 768], P('expert', None, 'dp')
- grad_up: bfloat16 [16, 2048, 768], P('expert', None, 'dp')
- grad_down: bfloat16 [16, 2048, 768], P('expert', None, 'dp')
- grad_tokens: bfloat16 [2048, 2048], P('expert')
Inputs may be any that keep to these rules, and one draw needn't show every extreme that they name: `route_ids`: among the 128 tokens of one device no expert is named more than 72 times, and in every draw some expert is named exactly 72 times by some device's tokens.
All inputs are finite; a program needn't handle non-finite values.
Results may differ from a plain program's by a relative error of at most 0.0065.
Values may be sent and summed in bfloat16 or wider, within the bound.
A program may use at most 128 MiB of HBM per device.

v0:
```python
import jax
import jax.numpy as jnp
from jax import lax
from jax.sharding import PartitionSpec as P


def on_device(tokens, out_grad, route_ids, route_probs, gate_store, up_store, down_store):
    tok_rows, model_width = tokens.shape
    top_count = route_ids.shape[1]
    experts = lax.axis_size("expert")
    capacity = max(2, 9 * tok_rows * top_count // (8 * experts))
    slot_total = tok_rows * top_count
    flat_ids = route_ids.reshape(-1)
    expert_range = jnp.arange(experts, dtype=jnp.int32)
    per_count = jnp.sum((flat_ids[:, None] == expert_range[None, :]).astype(jnp.int32), axis=0)
    offsets = jnp.cumsum(per_count) - per_count
    order = jnp.argsort(flat_ids, stable=True)
    sorted_ids = flat_ids[order]
    sorted_rank = jnp.arange(slot_total, dtype=jnp.int32) - offsets[sorted_ids]
    slot_rank = jnp.zeros((slot_total,), jnp.int32).at[order].set(sorted_rank)
    slot_place = flat_ids * capacity + slot_rank
    source = (
        jnp.full((experts * capacity,), slot_total, jnp.int32)
        .at[slot_place]
        .set(jnp.arange(slot_total, dtype=jnp.int32))
    )
    filled = source < slot_total
    safe_index = jnp.where(filled, source, 0)
    owner_row = safe_index // top_count
    x_slots = jnp.where(filled[:, None], tokens[owner_row], jnp.zeros((), jnp.bfloat16))
    slot_prob = jnp.where(filled, route_probs.reshape(-1)[safe_index], 0.0)
    dy_slots = (slot_prob[:, None] * out_grad[owner_row].astype(jnp.float32)).astype(jnp.bfloat16)
    x_slots = x_slots.reshape(experts, capacity, model_width)
    dy_slots = dy_slots.reshape(experts, capacity, model_width)
    gate_all, up_all, down_all = (
        lax.all_to_all(gate_store, "expert", split_axis=0, concat_axis=1, tiled=True),
        lax.all_to_all(up_store, "expert", split_axis=0, concat_axis=1, tiled=True),
        lax.all_to_all(down_store, "expert", split_axis=0, concat_axis=1, tiled=True),
    )
    gate_panel = gate_all[0]
    up_panel = up_all[0]
    col_width = model_width // lax.axis_size("dp")
    col_start = lax.axis_index("dp") * col_width
    x_part = lax.dynamic_slice_in_dim(x_slots, col_start, col_width, 2)
    dy_part = lax.dynamic_slice_in_dim(dy_slots, col_start, col_width, 2)
    x_sent, dy_sent = (
        lax.all_to_all(x_part, "expert", split_axis=0, concat_axis=0, tiled=True),
        lax.all_to_all(dy_part, "expert", split_axis=0, concat_axis=0, tiled=True),
    )
    x_in, dy_in = (
        lax.all_gather(x_sent, "dp", axis=2, tiled=True),
        lax.all_gather(dy_sent, "dp", axis=2, tiled=True),
    )
    rows_in = x_in.reshape(-1, model_width)
    dy_rows = dy_in.reshape(-1, model_width)
    gate_pre = jnp.dot(rows_in, gate_panel, preferred_element_type=jnp.float32)
    up_pre = jnp.dot(rows_in, up_panel, preferred_element_type=jnp.float32)
    sigmoid_gate = jax.nn.sigmoid(gate_pre)
    activation = (gate_pre * sigmoid_gate * up_pre).astype(jnp.bfloat16)
    down_panel = down_all[0]
    act_grad = jnp.dot(dy_rows, down_panel, preferred_element_type=jnp.float32)
    up_grad = (act_grad * gate_pre * sigmoid_gate).astype(jnp.bfloat16)
    gate_grad = (act_grad * up_pre * sigmoid_gate * (1.0 + gate_pre * (1.0 - sigmoid_gate))).astype(
        jnp.bfloat16
    )
    contract = (((0,), (0,)), ((), ()))
    grad_down = lax.dot_general(
        dy_rows, activation, contract, preferred_element_type=jnp.float32
    ).astype(jnp.bfloat16)
    grad_gate = lax.dot_general(
        rows_in, gate_grad, contract, preferred_element_type=jnp.float32
    ).astype(jnp.bfloat16)
    grad_up = lax.dot_general(
        rows_in, up_grad, contract, preferred_element_type=jnp.float32
    ).astype(jnp.bfloat16)
    back_contract = (((1,), (1,)), ((), ()))
    slot_half = lax.dot_general(
        gate_grad, gate_panel, back_contract, preferred_element_type=jnp.float32
    ) + lax.dot_general(up_grad, up_panel, back_contract, preferred_element_type=jnp.float32)
    summed = lax.psum_scatter(
        slot_half.reshape(experts, capacity, model_width), "dp", scatter_dimension=2, tiled=True
    )
    returned = lax.all_to_all(
        summed.astype(jnp.bfloat16), "expert", split_axis=0, concat_axis=0, tiled=True
    )
    share_width = returned.shape[2]
    slot_values = returned.reshape(experts * capacity, share_width)[slot_place]
    token_share = jnp.sum(
        slot_values.reshape(tok_rows, top_count, share_width).astype(jnp.float32), axis=1
    ).astype(jnp.bfloat16)
    grad_tokens = lax.all_gather(token_share, "dp", axis=1, tiled=True)
    return (grad_gate[None], grad_up[None], grad_down[None], grad_tokens)


def solution(mesh):
    return jax.shard_map(
        on_device,
        mesh=mesh,
        in_specs=(
            P("expert", None),
            P("expert", None),
            P("expert", None),
            P("expert", None),
            P(None, "expert", "dp"),
            P(None, "expert", "dp"),
            P(None, "expert", "dp"),
        ),
        out_specs=(
            P("expert", None, "dp"),
            P("expert", None, "dp"),
            P("expert", None, "dp"),
            P("expert", None),
        ),
        check_vma=False,
    )
```

profile of v0, /device:TPU:0, one launch (start us, length us, event | category | flops | bytes accessed | tf_op | source)
XLA Modules:
  0.0 365.0 jit_solution(2998000688810794630)
XLA Ops:
  7.2 8.5 %all-to-all-start.4 = ((bf16[16,128,384]{2,1,0:T(8,128)(2,1)}), bf16[16,128,384]{2,1,0:T(8,128)(2,1)S(1)}, u32[]{:S(2)}, u32[]{:S(2)}) async-start(bf16[16,128,384]{2,1,0:T(8,128)(2,1)} %param.11), calls=%async_computation.4 | async-start | bytes 3145728 | tf_op jit(solution)/shard_map/all_to_all | solution.py:36
  15.7 0.1 copy.15
  15.9 4.4 %sort.17 = (s32[1024]{0:T(1024)}, s32[1024]{0:T(1024)S(1)}) sort(s32[1024]{0:T(1024)S(1)} %reshape.99, s32[1024]{0:T(1024)S(1)} %iota.14), dimensions={0}, to_apply=%region_0.0 | sort | flops 10240 | bytes 16384 | tf_op jit(solution)/shard_map/jit(argsort)/sort | solution.py:17
  20.3 4.5 %gather_fusion = s32[1024]{0:T(1024)S(1)} fusion(s32[1024]{0:T(1024)S(1)} %reshape.99, s32[1024]{0:T(1024)S(1)} %get-tuple-element.23), kind=kCustom, calls=%fused_computation | custom fusion | bytes 12288 | tf_op jit(solution)/shard_map/gather | solution.py:18
  24.8 0.1 convert_reduce_fusion
  25.1 0.1 reduce.2
  25.2 0.7 fusion.12
  25.9 4.4 %compare_select_fusion.2 = (s32[1024,1]{0,1:T(1,128)S(1)}, s32[1024,1]{0,1:T(1,128)S(1)}) fusion(s32[]{:T(128)} %bitcast.11, s32[]{:T(128)} %bitcast.12, s32[]{:T(128)} %bitcast.13, s32[]{:T(128)} %bitcast.14, s32[]{:T(128)} %bitcast.15, s32[]{:T(128)} %bitcast.17, s32[]{:T(128)} %bitcast.16, s32[1024,1]{0,1:T(1,128)S(1)} %bitcast.63), kind=kLoop, calls=%fused_computation.36 | loop fusion | flops 15360 | bytes 12316 | tf_op jit(solution)/shard_map/gather | solution.py:19
  30.3 0.1 compare_reduce_fusion.8
  30.4 5.7 %select_subtract_fusion = s32[1024]{0:T(1024)S(1)} fusion(pred[1024]{0:T(1024)(128)(4,1)S(1)} %get-tuple-element.14, pred[1024]{0:T(1024)(128)(4,1)S(1)} %get-tuple-element.13, pred[1024]{0:T(1024)(128)(4,1)S(1)} %get-tuple-element.12, pred[1024]{0:T(1024)(128)(4,1)S(1)} %get-tuple-element.11, pred[1024]{0:T(1024)(128)(4,1)S(1)} %get-tuple-element.10, ...), kind=kLoop, calls=%fused_computation.54 | loop fusion | flops 10240 | bytes 17444 | tf_op jit(solution)/shard_map/sub | solution.py:19
  36.1 4.3 %scatter_custom_fusion = s32[1024]{0:T(1024)S(1)} fusion(s32[1024]{0:T(1024)S(1)} %get-tuple-element.24, s32[1024]{0:T(1024)S(1)} %select_subtract_fusion, s32[]{:T(128)} %constant.13.clone.1), kind=kCustom, calls=%fused_computation.61 | custom fusion | bytes 4100 | tf_op jit(solution)/shard_map/scatter | solution.py:20
  40.5 4.3 %scatter_custom_fusion.1 = s32[1152]{0:T(1024)S(1)} fusion(s32[1024]{0:T(1024)S(1)} %get-tuple-element.16, s32[1024]{0:T(1024)S(1)} %iota.16, s32[]{:T(128)} %constant.16.clone.1), kind=kCustom, calls=%fused_computation.57 | custom fusion | bytes 4612 | tf_op jit(solution)/shard_map/scatter | solution.py:25
  44.8 0.1 broadcast_in_dim.52
  44.9 5.9 %gather_fusion.1 = bf16[1152,2048]{1,0:T(8,128)(2,1)} fusion(bf16[128,2048]{1,0:T(8,128)(2,1)S(1)} %copy-done, s32[2048]{0:T(1024)S(1)} %pad_clamp_fusion.1), kind=kCustom, calls=%fused_computation.1 | custom fusion | bytes 9441792 | tf_op jit(solution)/shard_map/gather | solution.py:30
  50.9 3.6 dynamic-slice_select_fusion
  54.5 1.1 copy-done.4
  55.6 6.9 %all-to-all-start = ((bf16[16,72,1024]{2,1,0:T(8,128)(2,1)}), bf16[16,72,1024]{2,1,0:T(8,128)(2,1)S(1)}, u32[]{:S(2)}, u32[]{:S(2)}) async-start(bf16[16,72,1024]{2,1,0:T(8,128)(2,1)} %dynamic-slice_select_fusion), calls=%async_computation | async-start | bytes 4718592 | tf_op jit(solution)/shard_map/all_to_all | solution.py:47
  62.6 0.1 copy.17
  62.8 4.6 %gather_fusion.2 = f32[1152]{0:T(1024)S(1)} fusion(f32[1024]{0:T(1024)S(1)} %reshape.103, s32[2048]{0:T(1024)S(1)} %pad_clamp_fusion), kind=kCustom, calls=%fused_computation.2 | custom fusion | bytes 13824 | tf_op jit(solution)/shard_map/gather | solution.py:31
  67.5 5.9 %gather_fusion.3 = bf16[1152,2048]{1,0:T(8,128)(2,1)} fusion(bf16[128,2048]{1,0:T(8,128)(2,1)S(1)} %copy-done.2, s32[2048]{0:T(1024)S(1)} %pad_clamp_fusion.1), kind=kCustom, calls=%fused_computation.3 | custom fusion | bytes 9441792 | tf_op jit(solution)/shard_map/gather | solution.py:32
  73.4 3.6 fusion
  77.0 32.8 %all-to-all-done = bf16[16,72,1024]{2,1,0:T(8,128)(2,1)S(1)} async-done(((bf16[16,72,1024]{2,1,0:T(8,128)(2,1)}), bf16[16,72,1024]{2,1,0:T(8,128)(2,1)S(1)}, u32[]{:S(2)}, u32[]{:S(2)}) %all-to-all-start) | async-done | bytes 2359328 | tf_op jit(solution)/shard_map/all_to_all | solution.py:47
  109.7 1.4 copy-done.3
  111.1 11.0 %all-to-all-start.1 = ((bf16[16,72,1024]{2,1,0:T(8,128)(2,1)}), bf16[16,72,1024]{2,1,0:T(8,128)(2,1)}, u32[]{:S(2)}, u32[]{:S(2)}) async-start(bf16[16,72,1024]{2,1,0:T(8,128)(2,1)} %fusion), calls=%async_computation.1 | async-start | bytes 4718592 | tf_op jit(solution)/shard_map/all_to_all | solution.py:48
  122.1 0.7 all-gather.3.cloned.1.call-update
  122.8 46.4 %all-to-all-done.1 = bf16[16,72,1024]{2,1,0:T(8,128)(2,1)} async-done(((bf16[16,72,1024]{2,1,0:T(8,128)(2,1)}), bf16[16,72,1024]{2,1,0:T(8,128)(2,1)}, u32[]{:S(2)}, u32[]{:S(2)}) %all-to-all-start.1) | async-done | bytes 2359328 | tf_op jit(solution)/shard_map/all_to_all | solution.py:48
  169.2 10.9 %all-to-all-start.3 = ((bf16[16,128,384]{2,1,0:T(8,128)(2,1)}), bf16[16,128,384]{2,1,0:T(8,128)(2,1)S(1)}, u32[]{:S(2)}, u32[]{:S(2)}) async-start(bf16[16,128,384]{2,1,0:T(8,128)(2,1)} %param.12), calls=%async_computation.3 | async-start | bytes 3145728 | tf_op jit(solution)/shard_map/all_to_all | solution.py:37
  180.1 0.7 all-gather.5.cloned.1.call-update
  180.8 32.9 %all-to-all-done.3 = bf16[16,128,384]{2,1,0:T(8,128)(2,1)S(1)} async-done(((bf16[16,128,384]{2,1,0:T(8,128)(2,1)}), bf16[16,128,384]{2,1,0:T(8,128)(2,1)S(1)}, u32[]{:S(2)}, u32[]{:S(2)}) %all-to-all-start.3) | async-done | bytes 1572896 | tf_op jit(solution)/shard_map/all_to_all | solution.py:37
  213.7 7.4 %all-to-all-start.2 = ((bf16[16,128,384]{2,1,0:T(8,128)(2,1)}), bf16[16,128,384]{2,1,0:T(8,128)(2,1)}, u32[]{:S(2)}, u32[]{:S(2)}) async-start(bf16[16,128,384]{2,1,0:T(8,128)(2,1)} %param.13), calls=%async_computation.2 | async-start | bytes 3145728 | tf_op jit(solution)/shard_map/all_to_all | solution.py:38
  221.1 0.2 reduce-scatter.2.cloned.1.call-start
  221.4 6.8 %fusion.14 = f32[1152,384]{1,0:T(8,128)} fusion(bf16[1152,2048]{1,0:T(8,128)(2,1)} %bitcast.65, bf16[2048,384]{1,0:T(8,128)(2,1)} %bitcast.60), kind=kOutput, calls=%fused_computation.66 | convolution fusion | flops 1811939328 | bytes 8060928 | tf_op jit(solution)/shard_map/dot_general | solution.py:56
  228.2 3.9 %fusion.13 = f32[1152,384]{1,0:T(8,128)} fusion(bf16[1152,2048]{1,0:T(8,128)(2,1)S(1)} %bitcast.68, bf16[2048,384]{1,0:T(8,128)(2,1)S(1)} %bitcast.58), kind=kOutput, calls=%fused_computation.65 | convolution fusion | flops 1811939328 | bytes 8060928 | tf_op jit(solution)/shard_map/dot_general | solution.py:57
  232.1 22.7 %all-to-all-done.2 = bf16[16,128,384]{2,1,0:T(8,128)(2,1)} async-done(((bf16[16,128,384]{2,1,0:T(8,128)(2,1)}), bf16[16,128,384]{2,1,0:T(8,128)(2,1)}, u32[]{:S(2)}, u32[]{:S(2)}) %all-to-all-start.2) | async-done | bytes 1572896 | tf_op jit(solution)/shard_map/all_to_all | solution.py:38
  254.8 7.0 %multiply_convert_fusion.1 = (bf16[1152,384]{1,0:T(8,128)(2,1)S(1)}, bf16[1152,384]{1,0:T(8,128)(2,1)S(1)}) fusion(f32[1152,384]{1,0:T(8,128)} %fusion.14, f32[1152,384]{1,0:T(8,128)} %fusion.13, bf16[1152,2048]{1,0:T(8,128)(2,1)} %bitcast.69, bf16[2048,384]{1,0:T(8,128)(2,1)} %bitcast.23), kind=kOutput, calls=%fused_computation.19 | convolution fusion | flops 1817690112 | bytes 11599872 | tf_op jit(solution)/shard_map/dot_general | solution.py:61
  261.8 2.7 fusion.15
  264.5 5.1 %convolution_add_fusion = f32[1152,2048]{1,0:T(8,128)} fusion(f32[1152,2048]{1,0:T(8,128)S(1)} %fusion.15, bf16[1152,384]{1,0:T(8,128)(2,1)S(1)} %get-tuple-element.21, bf16[2048,384]{1,0:T(8,128)(2,1)S(1)} %bitcast.59), kind=kOutput, calls=%fused_computation.7 | convolution fusion | flops 1814298624 | bytes 21331968 | tf_op jit(solution)/shard_map/dot_general | solution.py:79
  269.6 18.8 %reduce-scatter.2.cloned.1.call-done = f32[16,72,1024]{2,1,0:T(8,128)} async-done(((f32[16,72,2048]{2,1,0:T(8,128)}), f32[16,72,1024]{2,1,0:T(8,128)}) %reduce-scatter.2.cloned.1.call-update) | async-done | bytes 4718608 | tf_op jit(solution)/shard_map/reduce_scatter | solution.py:80
  288.5 4.1 %convert_element_type.47 = bf16[16,72,1024]{2,1,0:T(8,128)(2,1)} convert(f32[16,72,1024]{2,1,0:T(8,128)} %reduce-scatter.2.cloned.1.call-done) | non-fusion elementwise | flops 1179648 | bytes 7077888 | tf_op jit(solution)/shard_map/convert_element_type | solution.py:84
  292.6 6.9 %all-to-all-start.5 = ((bf16[16,72,1024]{2,1,0:T(8,128)(2,1)}), bf16[16,72,1024]{2,1,0:T(8,128)(2,1)S(1)}, u32[]{:S(2)}, u32[]{:S(2)}) async-start(bf16[16,72,1024]{2,1,0:T(8,128)(2,1)} %convert_element_type.47), calls=%async_computation.6 | async-start | bytes 4718592 | tf_op jit(solution)/shard_map/all_to_all | solution.py:83
  299.6 6.7 %fusion.2 = bf16[1,2048,384]{2,1,0:T(8,128)(2,1)} fusion(bf16[1152,2048]{1,0:T(8,128)(2,1)} %bitcast.66, bf16[1152,384]{1,0:T(8,128)(2,1)} %copy-done.6), kind=kOutput, calls=%fused_computation.14 | convolution fusion | flops 1812725760 | bytes 7176192 | tf_op jit(solution)/shard_map/dot_general | solution.py:73
  306.3 6.5 %fusion.1 = bf16[1,2048,384]{2,1,0:T(8,128)(2,1)} fusion(bf16[1152,2048]{1,0:T(8,128)(2,1)} %bitcast.67, bf16[1152,384]{1,0:T(8,128)(2,1)S(1)} %copy-done.8), kind=kOutput, calls=%fused_computation.13 | convolution fusion | flops 1812725760 | bytes 7176192 | tf_op jit(solution)/shard_map/dot_general | solution.py:70
  312.8 4.0 %fusion.3 = bf16[1,2048,384]{2,1,0:T(8,128)(2,1)} fusion(bf16[1152,2048]{1,0:T(8,128)(2,1)S(1)} %bitcast.72, f32[1152,384]{1,0:T(8,128)S(1)} %copy-done.13, f32[1152,384]{1,0:T(8,128)S(1)} %copy-done.12), kind=kOutput, calls=%fused_computation.15 | convolution fusion | flops 1815379968 | bytes 9830400 | tf_op jit(solution)/shard_map/dot_general | solution.py:67
  316.8 30.4 %all-to-all-done.5 = bf16[16,72,1024]{2,1,0:T(8,128)(2,1)S(1)} async-done(((bf16[16,72,1024]{2,1,0:T(8,128)(2,1)}), bf16[16,72,1024]{2,1,0:T(8,128)(2,1)S(1)}, u32[]{:S(2)}, u32[]{:S(2)}) %all-to-all-start.5) | async-done | bytes 2359328 | tf_op jit(solution)/shard_map/all_to_all | solution.py:83
  347.1 5.4 %gather_fusion.4 = bf16[1024,1024]{1,0:T(8,128)(2,1)} fusion(bf16[1152,1024]{1,0:T(8,128)(2,1)S(1)} %bitcast.54, s32[1024]{0:T(1024)S(1)} %get-tuple-element.15), kind=kCustom, calls=%fused_computation.4 | custom fusion | bytes 4198400 | tf_op jit(solution)/shard_map/gather | solution.py:87
  352.5 3.0 bitcast_reduce_fusion
  355.5 2.2 all_gather.11
  357.7 0.8 copy.19
  (52 shorter events, 0.6 us)
Async XLA Ops:
  7.2 37.8 %copy-start = (bf16[128,2048]{1,0:T(8,128)(2,1)S(1)}, bf16[128,2048]{1,0:T(8,128)(2,1)}, u32[]{:S(2)}) copy-start(bf16[128,2048]{1,0:T(8,128)(2,1)} %param.7) | copy-start | bytes 1572868
  7.2 8.5 %copy-start.9 = (s32[128,8]{0,1:T(8,128)S(1)}, s32[128,8]{0,1:T(8,128)}, u32[]{:S(2)}) copy-start(s32[128,8]{0,1:T(8,128)} %param.9) | copy-start | bytes 12292
  7.2 47.3 %all-to-all-start.4 = ((bf16[16,128,384]{2,1,0:T(8,128)(2,1)}), bf16[16,128,384]{2,1,0:T(8,128)(2,1)S(1)}, u32[]{:S(2)}, u32[]{:S(2)}) async-start(bf16[16,128,384]{2,1,0:T(8,128)(2,1)} %param.11), calls=%async_computation.4 | async-start | bytes 3145728 | tf_op jit(solution)/shard_map/all_to_all | solution.py:36
  54.5 8.1 %copy-start.10 = (f32[128,8]{0,1:T(8,128)S(1)}, f32[128,8]{0,1:T(8,128)}, u32[]{:S(2)}) copy-start(f32[128,8]{0,1:T(8,128)} %param.10) | copy-start | bytes 12292
  54.5 1.1 copy-start.4
  55.6 54.1 %all-to-all-start = ((bf16[16,72,1024]{2,1,0:T(8,128)(2,1)}), bf16[16,72,1024]{2,1,0:T(8,128)(2,1)S(1)}, u32[]{:S(2)}, u32[]{:S(2)}) async-start(bf16[16,72,1024]{2,1,0:T(8,128)(2,1)} %dynamic-slice_select_fusion), calls=%async_computation | async-start | bytes 4718592 | tf_op jit(solution)/shard_map/all_to_all | solution.py:47
  62.8 4.7 %copy-start.2 = (bf16[128,2048]{1,0:T(8,128)(2,1)S(1)}, bf16[128,2048]{1,0:T(8,128)(2,1)}, u32[]{:S(2)}) copy-start(bf16[128,2048]{1,0:T(8,128)(2,1)} %param.8) | copy-start | bytes 1572868
  109.7 1.4 copy-start.3
  111.1 58.1 %all-to-all-start.1 = ((bf16[16,72,1024]{2,1,0:T(8,128)(2,1)}), bf16[16,72,1024]{2,1,0:T(8,128)(2,1)}, u32[]{:S(2)}, u32[]{:S(2)}) async-start(bf16[16,72,1024]{2,1,0:T(8,128)(2,1)} %fusion), calls=%async_computation.1 | async-start | bytes 4718592 | tf_op jit(solution)/shard_map/all_to_all | solution.py:48
  122.1 99.2 %all-gather.3.cloned.1.call-start = ((), (), s32[]{:S(2)}) async-start(), calls=%async_computation.7 | async-start | bytes 7077888 | tf_op jit(solution)/shard_map/all_gather | solution.py:51
  169.2 44.5 %all-to-all-start.3 = ((bf16[16,128,384]{2,1,0:T(8,128)(2,1)}), bf16[16,128,384]{2,1,0:T(8,128)(2,1)S(1)}, u32[]{:S(2)}, u32[]{:S(2)}) async-start(bf16[16,128,384]{2,1,0:T(8,128)(2,1)} %param.12), calls=%async_computation.3 | async-start | bytes 3145728 | tf_op jit(solution)/shard_map/all_to_all | solution.py:37
  180.1 74.7 %all-gather.5.cloned.1.call-start = ((), (), s32[]{:S(2)}) async-start(), calls=%async_computation.8 | async-start | bytes 7077888 | tf_op jit(solution)/shard_map/all_gather | solution.py:52
  213.7 41.1 %all-to-all-start.2 = ((bf16[16,128,384]{2,1,0:T(8,128)(2,1)}), bf16[16,128,384]{2,1,0:T(8,128)(2,1)}, u32[]{:S(2)}, u32[]{:S(2)}) async-start(bf16[16,128,384]{2,1,0:T(8,128)(2,1)} %param.13), calls=%async_computation.2 | async-start | bytes 3145728 | tf_op jit(solution)/shard_map/all_to_all | solution.py:38
  221.1 67.4 %reduce-scatter.2.cloned.1.call-start = ((), (), s32[]{:S(2)}) async-start(), calls=%async_computation.9 | async-start | bytes 14155776 | tf_op jit(solution)/shard_map/reduce_scatter | solution.py:80
  221.3 6.8 %copy-start.11 = (bf16[16,72,2048]{2,1,0:T(8,128)(2,1)S(1)}, bf16[16,72,2048]{2,1,0:T(8,128)(2,1)}, u32[]{:S(2)}) copy-start(bf16[16,72,2048]{2,1,0:T(8,128)(2,1)} %all-gather.3.cloned.1.call-done) | copy-start | bytes 14155780
  254.8 7.1 %copy-start.5 = (bf16[16,128,384]{2,1,0:T(8,128)(2,1)S(1)}, bf16[16,128,384]{2,1,0:T(8,128)(2,1)}, u32[]{:S(2)}) copy-start(bf16[16,128,384]{2,1,0:T(8,128)(2,1)} %copy-done.4) | copy-start | bytes 4718596
  261.8 2.7 copy-start.7
  261.8 2.7 copy-start.6
  292.6 54.6 %all-to-all-start.5 = ((bf16[16,72,1024]{2,1,0:T(8,128)(2,1)}), bf16[16,72,1024]{2,1,0:T(8,128)(2,1)S(1)}, u32[]{:S(2)}, u32[]{:S(2)}) async-start(bf16[16,72,1024]{2,1,0:T(8,128)(2,1)} %convert_element_type.47), calls=%async_computation.6 | async-start | bytes 4718592 | tf_op jit(solution)/shard_map/all_to_all | solution.py:83
  299.5 6.7 %copy-start.8 = (bf16[1152,384]{1,0:T(8,128)(2,1)S(1)}, bf16[1152,384]{1,0:T(8,128)(2,1)}, u32[]{:S(2)}) copy-start(bf16[1152,384]{1,0:T(8,128)(2,1)} %copy-done.7) | copy-start | bytes 2654212
  299.5 13.2 %slice-start = ((s8[4718592]{0:T(1024)(128)(4,1)}), s8[4194304]{0:T(1024)(128)(4,1)S(1)}, s32[]{:S(2)}) async-start(s8[4718592]{0:T(1024)(128)(4,1)} %bitcast.70), calls=%async_computation.10 | async-start | bytes 8388608
  306.3 6.5 %slice-start.1 = ((s8[4718592]{0:T(1024)(128)(4,1)}), s8[524288]{0:T(1024)(128)(4,1)S(1)}, s32[]{:S(2)}) async-start(s8[4718592]{0:T(1024)(128)(4,1)} %bitcast.70), calls=%async_computation.11 | async-start | bytes 1048576
  306.3 6.5 %copy-start.12 = (f32[1152,384]{1,0:T(8,128)S(1)}, f32[1152,384]{1,0:T(8,128)}, u32[]{:S(2)}) copy-start(f32[1152,384]{1,0:T(8,128)} %fusion.14) | copy-start | bytes 5308420
  306.3 6.5 %copy-start.13 = (f32[1152,384]{1,0:T(8,128)S(1)}, f32[1152,384]{1,0:T(8,128)}, u32[]{:S(2)}) copy-start(f32[1152,384]{1,0:T(8,128)} %fusion.13) | copy-start | bytes 5308420
  347.1 11.4 %copy-start.1 = (bf16[128,2048]{1,0:T(8,128)(2,1)S(1)}, bf16[128,2048]{1,0:T(8,128)(2,1)}, u32[]{:S(2)}) copy-start(bf16[128,2048]{1,0:T(8,128)(2,1)} %param.7) | copy-start | bytes 1572868
Sparse Core Ops, SparseCore 0:
  124.4 15.6 all-gather.2
  182.4 15.7 all-gather.4
  269.7 18.6 reduce-scatter.1
where the time goes:
time: 371 us; the launch traced here: 365 us
  waiting for transfers between devices  185 us (50%)
  starting transfers between devices  51.8 us (14%)
  matrix products  42.7 us (12%)
  local copies, waits for them, and re-layouts  39.7 us (11%)
  other arithmetic  29.2 us (8%)
  between operations  14.1 us (4%)
    all_to_all x1, waiting for transfers between devices, on_device(): lax.all_to_all(dy_part, 'expert', split_axis=0, concat_axis=0, tiled=True)  46.4 us
    all_to_all x1, waiting for transfers between devices, on_device(): lax.all_to_all(up_store, 'expert', split_axis=0, concat_axis=1, tiled=True)  32.9 us
    all_to_all x1, waiting for transfers between devices, on_device(): lax.all_to_all(x_part, 'expert', split_axis=0, concat_axis=0, tiled=True)  32.8 us
    all_to_all x1, waiting for transfers between devices, on_device(): lax.all_to_all(summed.astype(jnp.bfloat16), 'expert', split_axis=0, conca...  30.4 us
    all_to_all x1, waiting for transfers between devices, on_device(): lax.all_to_all(down_store, 'expert', split_axis=0, concat_axis=1, tiled=T...  22.7 us
    reduce_scatter x1, waiting for transfers between devices, on_device(): lax.psum_scatter(slot_half.reshape(experts, capacity, model_width), 'dp',...  18.8 us
    all_to_all x1, starting transfers between devices, on_device(): lax.all_to_all(dy_part, 'expert', split_axis=0, concat_axis=0, tiled=True)  11 us
    all_to_all x1, starting transfers between devices, on_device(): lax.all_to_all(up_store, 'expert', split_axis=0, concat_axis=1, tiled=True)  10.9 us
  transfers between devices with their start and end apart: 9, of which 6 were waited for; matrix products, arithmetic and copies ran while one was open for 22% of the time, Pallas kernels for 0%

commit v1 on v0

--- a/solution.py
+++ b/solution.py
@@ -92,9 +92,51 @@
     return (grad_gate[None], grad_up[None], grad_down[None], grad_tokens)
 
 
+def gathered(tokens, out_grad, route_ids, route_probs, gate_store, up_store, down_store):
+    tok_rows, model_width = tokens.shape
+    experts = lax.axis_size("expert")
+    half = tok_rows // lax.axis_size("dp")
+    start = lax.axis_index("dp") * half
+    both = ("expert", "dp")
+    chosen = route_ids[:, :, None] == jnp.arange(experts, dtype=jnp.int32)[None, None, :]
+    weight = jnp.sum(jnp.where(chosen, route_probs[:, :, None], 0.0), axis=1)
+    weight = lax.all_to_all(weight.T.reshape(experts, tok_rows), "expert", split_axis=0, concat_axis=0, tiled=True)
+    weight = weight.reshape(-1, 1)
+    x_all = lax.all_gather(lax.dynamic_slice_in_dim(tokens, start, half, 0), both, axis=0, tiled=True)
+    g_all = lax.all_gather(lax.dynamic_slice_in_dim(out_grad, start, half, 0), both, axis=0, tiled=True)
+    gate_panel, up_panel, down_panel = (
+        lax.all_to_all(store, "expert", split_axis=0, concat_axis=1, tiled=True)[0]
+        for store in (gate_store, up_store, down_store)
+    )
+    gate_pre = jnp.dot(x_all, gate_panel, preferred_element_type=jnp.float32)
+    up_pre = jnp.dot(x_all, up_panel, preferred_element_type=jnp.float32)
+    act_grad = jnp.dot(g_all, down_panel, preferred_element_type=jnp.float32) * weight
+    sig = jax.nn.sigmoid(gate_pre)
+    activation = (gate_pre * sig * up_pre * weight).astype(jnp.bfloat16)
+    up_grad = (act_grad * gate_pre * sig).astype(jnp.bfloat16)
+    gate_grad = (act_grad * up_pre * sig * (1.0 + gate_pre * (1.0 - sig))).astype(jnp.bfloat16)
+    back = (((1,), (1,)), ((), ()))
+    slot_half = lax.dot_general(gate_grad, gate_panel, back, preferred_element_type=jnp.float32) + lax.dot_general(
+        up_grad, up_panel, back, preferred_element_type=jnp.float32
+    )
+    share = lax.psum_scatter(slot_half.astype(jnp.bfloat16), both, scatter_dimension=0, tiled=True)
+    grad_tokens = lax.all_gather(share, "dp", axis=0, tiled=True)
+    outer = (((0,), (0,)), ((), ()))
+    grad_down = lax.dot_general(g_all, activation, outer, preferred_element_type=jnp.float32).astype(jnp.bfloat16)
+    grad_gate = lax.dot_general(x_all, gate_grad, outer, preferred_element_type=jnp.float32).astype(jnp.bfloat16)
+    grad_up = lax.dot_general(x_all, up_grad, outer, preferred_element_type=jnp.float32).astype(jnp.bfloat16)
+    return (grad_gate[None], grad_up[None], grad_down[None], grad_tokens)
+
+
+def choose(tokens, out_grad, route_ids, *rest):
+    if lax.axis_size("expert") <= 2 * route_ids.shape[1]:
+        return gathered(tokens, out_grad, route_ids, *rest)
+    return on_device(tokens, out_grad, route_ids, *rest)
+
+
 def solution(mesh):
     return jax.shard_map(
-        on_device,
+        choose,
         mesh=mesh,
         in_specs=(
             P("expert", None),

time: 371 us -> 415 us (1.12); the launches traced: 365 us -> 414 us
  blocking collectives: 2.18 us -> 127 us
  starting transfers between devices: 51.8 us -> 4.7 us
  local copies, waits for them, and re-layouts: 39.7 us -> 5.61 us
  matrix products: 42.7 us -> 71.2 us
  other arithmetic: 29.2 us -> 0.84 us
  waiting for transfers between devices: 185 us -> 191 us
    all_to_all x6 -> x1, waiting for transfers between devices: 165 us -> 30.6 us  [gathered(): lax.all_to_all(store, 'expert', split_axis=0, concat_axis=1, tiled=True)[0]]
    all_to_all x0 -> x3, blocking collectives: none -> 125 us  [the longest x2 109 us: gathered(): lax.all_to_all(store, 'expert', split_axis=0, concat_axis=1, tiled=True)[0]]
    reduce_scatter x1, waiting for transfers between devices: 18.8 us -> 123 us  [gathered(): lax.psum_scatter(slot_half.astype(jnp.bfloat16), both, scatter_dimension=...]
    all_to_all x6 -> x1, starting transfers between devices: 51.5 us -> 4.58 us  [gathered(): lax.all_to_all(store, 'expert', split_axis=0, concat_axis=1, tiled=True)[0]]
    all_gather x2, waiting for transfers between devices: 0.02 us -> 37.2 us  [the longest x1 37.2 us: gathered(): lax.all_gather(lax.dynamic_slice_in_dim(out_grad, start, half, 0), both,...]
    dot_general x8, matrix products: 42.7 us -> 71.2 us  [the longest x1 11.5 us: gathered(): jnp.dot(g_all, down_panel, preferred_element_type=jnp.float32) * weight]
    gather x6 -> x0, local copies, waits for them, and re-layouts: 27 us -> none  [the longest x1 5.94 us: on_device(): tokens[owner_row]]
    scatter x2 -> x0, local copies, waits for them, and re-layouts: 8.63 us -> none  [the longest x1 4.32 us: on_device(): source = jnp.full((experts * capacity,), slot_total, jnp.int32).at[slot_p...]
  transfers between devices with their start and end apart: 9 -> 4, of which waited for: 6 -> 3; matrix products, arithmetic and copies ran while one was open for 22% -> 11% of each run, Pallas kernels for 0% -> 0%
where the time goes in v1:
time: 415 us; the launch traced here: 414 us
  waiting for transfers between devices  191 us (46%)
  blocking collectives  127 us (31%)
  matrix products  71.2 us (17%)
  between operations  13.9 us (3%)
  local copies, waits for them, and re-layouts  5.61 us (1%)
  starting transfers between devices  4.7 us (1%)
    reduce_scatter x1, waiting for transfers between devices, gathered(): lax.psum_scatter(slot_half.astype(jnp.bfloat16), both, scatter_dimension=...  123 us
    all_to_all x2, blocking collectives, gathered(): lax.all_to_all(store, 'expert', split_axis=0, concat_axis=1, tiled=True)[0]  109 us
    all_gather x1, waiting for transfers between devices, gathered(): lax.all_gather(lax.dynamic_slice_in_dim(out_grad, start, half, 0), both,...  37.2 us
    all_to_all x1, waiting for transfers between devices, gathered(): lax.all_to_all(store, 'expert', split_axis=0, concat_axis=1, tiled=True)[0]  30.6 us
    all_to_all x1, blocking collectives, gathered(): lax.all_to_all(weight.T.reshape(experts, tok_rows), 'expert', split_axis=...  15.4 us
    dot_general x1, matrix products, gathered(): jnp.dot(g_all, down_panel, preferred_element_type=jnp.float32) * weight  11.5 us
    dot_general x1, matrix products, gathered(): lax.dot_general(up_grad, up_panel, back, preferred_element_type=jnp.float32)  10.3 us
    dot_general x1, matrix products, gathered(): gate_pre = jnp.dot(x_all, gate_panel, preferred_element_type=jnp.float32)  10.2 us
  transfers between devices with their start and end apart: 4, of which 3 were waited for; matrix products, arithmetic and copies ran while one was open for 11% of the time, Pallas kernels for 0%

profile of v1, /device:TPU:0, one launch (start us, length us, event | category | flops | bytes accessed | tf_op | source)
XLA Modules:
  0.0 414.2 jit_solution(4239823326702032732)
XLA Ops:
  7.2 0.0 copy-start
  7.2 0.0 all-gather.3.cloned.1.call-start
  7.2 1.0 copy-done
  8.2 0.7 constant_dynamic-slice_fusion.1
  8.9 0.0 all-gather.3.cloned.1.call-update
  9.0 0.0 all-gather.5.cloned.1.call-start
  9.0 1.7 constant_dynamic-slice_fusion
  10.7 0.0 all-gather.5.cloned.1.call-update
  10.7 0.0 copy-start.7
  10.7 0.8 select_reduce_fusion
  11.6 15.4 %all_to_all.36 = f32[16,1,128]{2,1,0:T(1,128)S(1)} all-to-all(f32[16,1,128]{2,1,0:T(1,128)S(1)} %bitcast.34), channel_id=1, replica_groups=mesh['dp'=2,'expert'=16] {'expert'}, dimensions={0} | all-to-all | bytes 16384 | tf_op jit(solution)/shard_map/all_to_all | solution.py:103
  27.0 52.7 %all_to_all.37 = bf16[16,128,384]{2,1,0:T(8,128)(2,1)} all-to-all(bf16[16,128,384]{2,1,0:T(8,128)(2,1)} %param.11), channel_id=1, replica_groups=mesh['dp'=2,'expert'=16] {'expert'}, dimensions={0} | all-to-all | bytes 3145728 | tf_op jit(solution)/shard_map/all_to_all | solution.py:108
  79.7 0.0 copy-done.7
  79.7 56.4 %all_to_all.38 = bf16[16,128,384]{2,1,0:T(8,128)(2,1)S(1)} all-to-all(bf16[16,128,384]{2,1,0:T(8,128)(2,1)S(1)} %copy-done.7), channel_id=1, replica_groups=mesh['dp'=2,'expert'=16] {'expert'}, dimensions={0} | all-to-all | bytes 3145728 | tf_op jit(solution)/shard_map/all_to_all | solution.py:108
  136.1 4.6 %all-to-all-start = ((bf16[16,128,384]{2,1,0:T(8,128)(2,1)}), bf16[16,128,384]{2,1,0:T(8,128)(2,1)}, u32[]{:S(2)}, u32[]{:S(2)}) async-start(bf16[16,128,384]{2,1,0:T(8,128)(2,1)} %param.13), calls=%async_computation | async-start | bytes 3145728 | tf_op jit(solution)/shard_map/all_to_all | solution.py:108
  140.7 0.0 reduce-scatter.2.cloned.1.call-start
  140.8 0.0 all-gather.3.cloned.1.call-done
  140.8 0.0 copy-start.8
  140.8 10.2 %fusion.7 = f32[2048,384]{1,0:T(8,128)} fusion(bf16[2048,2048]{1,0:T(8,128)(2,1)} %all-gather.3.cloned.1.call-done, bf16[2048,384]{1,0:T(8,128)(2,1)} %bitcast.32), kind=kOutput, calls=%fused_computation.20 | convolution fusion | flops 3221225472 | bytes 13107200 | tf_op jit(solution)/shard_map/dot_general | solution.py:111
  151.0 0.0 copy-done.8
  151.0 6.4 %fusion.6 = f32[2048,384]{1,0:T(8,128)} fusion(bf16[2048,2048]{1,0:T(8,128)(2,1)S(1)} %copy-done.8, bf16[2048,384]{1,0:T(8,128)(2,1)S(1)} %bitcast.30), kind=kOutput, calls=%fused_computation.19 | convolution fusion | flops 3221225472 | bytes 13107200 | tf_op jit(solution)/shard_map/dot_general | solution.py:112
  157.3 30.6 %all-to-all-done = bf16[16,128,384]{2,1,0:T(8,128)(2,1)} async-done(((bf16[16,128,384]{2,1,0:T(8,128)(2,1)}), bf16[16,128,384]{2,1,0:T(8,128)(2,1)}, u32[]{:S(2)}, u32[]{:S(2)}) %all-to-all-start) | async-done | bytes 1572896 | tf_op jit(solution)/shard_map/all_to_all | solution.py:108
  187.9 37.2 %all-gather.5.cloned.1.call-done = bf16[2048,2048]{1,0:T(8,128)(2,1)} async-done(((bf16[64,2048]{1,0:T(8,128)(2,1)}), bf16[2048,2048]{1,0:T(8,128)(2,1)}) %all-gather.5.cloned.1.call-update) | async-done | bytes 8388624 | tf_op jit(solution)/shard_map/all_gather | solution.py:106
  225.1 0.0 copy-start.2
  225.1 11.5 %multiply_convert_fusion.1 = (bf16[2048,384]{1,0:T(8,128)(2,1)S(1)}, bf16[2048,384]{1,0:T(8,128)(2,1)S(1)}) fusion(f32[2048,384]{1,0:T(8,128)} %fusion.7, f32[2048,384]{1,0:T(8,128)} %fusion.6, f32[2048]{0:T(1024)S(1)} %bitcast.35, bf16[2048,2048]{1,0:T(8,128)(2,1)} %all-gather.5.cloned.1.call-done, bf16[2048,384]{1,0:T(8,128)(2,1)} %bitcast), kind=kOutput, calls=%fused_computation.2 | convolution fusion | flops 3232235520 | bytes 19406848 | tf_op jit(solution)/shard_map/dot_general | solution.py:113
  236.7 0.0 copy-start.3
  236.7 0.0 copy-start.5
  236.7 0.0 copy-done.2
  236.7 8.2 %fusion.8 = f32[2048,2048]{1,0:T(8,128)} fusion(bf16[2048,384]{1,0:T(8,128)(2,1)S(1)} %get-tuple-element.5, bf16[2048,384]{1,0:T(8,128)(2,1)S(1)} %bitcast.33), kind=kOutput, calls=%fused_computation.21 | convolution fusion | flops 3221225472 | bytes 19922944 | tf_op jit(solution)/shard_map/dot_general | solution.py:119
  244.9 0.0 copy-done.3
  244.9 0.0 copy-done.5
  244.9 10.3 %add_convert_fusion = bf16[2048,2048]{1,0:T(8,128)(2,1)} fusion(f32[2048,2048]{1,0:T(8,128)} %fusion.8, bf16[2048,384]{1,0:T(8,128)(2,1)S(1)} %get-tuple-element.4, bf16[2048,384]{1,0:T(8,128)(2,1)S(1)} %bitcast.31), kind=kOutput, calls=%fused_computation | convolution fusion | flops 3229614080 | bytes 28311552 | tf_op jit(solution)/shard_map/dot_general | solution.py:119
  255.2 0.0 copy-start.6
  255.2 0.0 reduce-scatter.2.cloned.1.call-update
  255.2 1.4 copy-done.6
  256.6 9.3 %fusion.1 = bf16[1,2048,384]{2,1,0:T(8,128)(2,1)} fusion(bf16[2048,2048]{1,0:T(8,128)(2,1)} %all-gather.3.cloned.1.call-done, bf16[2048,384]{1,0:T(8,128)(2,1)S(1)} %copy-done.6), kind=kOutput, calls=%fused_computation.10 | convolution fusion | flops 3222011904 | bytes 11534336 | tf_op jit(solution)/shard_map/dot_general | solution.py:127
  266.0 0.0 copy-done.4
  266.0 9.4 %fusion = bf16[1,2048,384]{2,1,0:T(8,128)(2,1)} fusion(bf16[2048,2048]{1,0:T(8,128)(2,1)} %all-gather.3.cloned.1.call-done, bf16[2048,384]{1,0:T(8,128)(2,1)S(1)} %copy-done.4), kind=kOutput, calls=%fused_computation.9 | convolution fusion | flops 3222011904 | bytes 11534336 | tf_op jit(solution)/shard_map/dot_general | solution.py:126
  275.3 0.0 slice-done
  275.3 0.0 slice-done.1
  275.3 0.0 copy-done.9
  275.3 0.0 copy-done.10
  275.4 0.0 copy-start.1
  275.4 6.0 %fusion.2 = bf16[1,2048,384]{2,1,0:T(8,128)(2,1)} fusion(bf16[2048,2048]{1,0:T(8,128)(2,1)S(1)} %bitcast.38, f32[2048,384]{1,0:T(8,128)S(1)} %copy-done.10, f32[2048,384]{1,0:T(8,128)S(1)} %copy-done.9, f32[2048]{0:T(1024)S(1)} %bitcast.36), kind=kOutput, calls=%fused_computation.11 | convolution fusion | flops 3227516928 | bytes 16261120 | tf_op jit(solution)/shard_map/dot_general | solution.py:125
  281.4 123.1 %reduce-scatter.2.cloned.1.call-done = bf16[64,2048]{1,0:T(8,128)(2,1)} async-done(((bf16[2048,2048]{1,0:T(8,128)(2,1)}), bf16[64,2048]{1,0:T(8,128)(2,1)}) %reduce-scatter.2.cloned.1.call-update) | async-done | bytes 262160 | tf_op jit(solution)/shard_map/reduce_scatter | solution.py:122
  404.5 2.4 all_gather.11
  406.8 0.8 copy.19
  407.6 0.0 copy-done.1
  (6 shorter events, 0.0 us)
Async XLA Ops:
  7.2 1.1 copy-start
  7.2 133.6 %all-gather.3.cloned.1.call-start = ((), (), s32[]{:S(2)}) async-start(), calls=%async_computation.5 | async-start | bytes 8650752 | tf_op jit(solution)/shard_map/all_gather | solution.py:105
  9.0 216.2 %all-gather.5.cloned.1.call-start = ((), (), s32[]{:S(2)}) async-start(), calls=%async_computation.6 | async-start | bytes 8650752 | tf_op jit(solution)/shard_map/all_gather | solution.py:106
  10.7 69.0 %copy-start.7 = (bf16[16,128,384]{2,1,0:T(8,128)(2,1)S(1)}, bf16[16,128,384]{2,1,0:T(8,128)(2,1)}, u32[]{:S(2)}) copy-start(bf16[16,128,384]{2,1,0:T(8,128)(2,1)} %param.12) | copy-start | bytes 4718596
  136.1 51.8 %all-to-all-start = ((bf16[16,128,384]{2,1,0:T(8,128)(2,1)}), bf16[16,128,384]{2,1,0:T(8,128)(2,1)}, u32[]{:S(2)}, u32[]{:S(2)}) async-start(bf16[16,128,384]{2,1,0:T(8,128)(2,1)} %param.13), calls=%async_computation | async-start | bytes 3145728 | tf_op jit(solution)/shard_map/all_to_all | solution.py:108
  140.7 263.7 %reduce-scatter.2.cloned.1.call-start = ((), (), s32[]{:S(2)}) async-start(), calls=%async_computation.7 | async-start | bytes 8650752 | tf_op jit(solution)/shard_map/reduce_scatter | solution.py:122
  140.8 10.2 %copy-start.8 = (bf16[2048,2048]{1,0:T(8,128)(2,1)S(1)}, bf16[2048,2048]{1,0:T(8,128)(2,1)}, u32[]{:S(2)}) copy-start(bf16[2048,2048]{1,0:T(8,128)(2,1)} %all-gather.3.cloned.1.call-done) | copy-start | bytes 25165828
  225.1 11.6 %copy-start.2 = (bf16[16,128,384]{2,1,0:T(8,128)(2,1)S(1)}, bf16[16,128,384]{2,1,0:T(8,128)(2,1)}, u32[]{:S(2)}) copy-start(bf16[16,128,384]{2,1,0:T(8,128)(2,1)} %all_to_all.37) | copy-start | bytes 4718596
  236.7 8.2 %copy-start.3 = (bf16[2048,384]{1,0:T(8,128)(2,1)}, bf16[2048,384]{1,0:T(8,128)(2,1)S(1)}, u32[]{:S(2)}) copy-start(bf16[2048,384]{1,0:T(8,128)(2,1)S(1)} %get-tuple-element.5) | copy-start | bytes 4718596
  236.7 8.2 %copy-start.5 = (bf16[2048,384]{1,0:T(8,128)(2,1)}, bf16[2048,384]{1,0:T(8,128)(2,1)S(1)}, u32[]{:S(2)}) copy-start(bf16[2048,384]{1,0:T(8,128)(2,1)S(1)} %get-tuple-element.4) | copy-start | bytes 4718596
  255.2 1.4 copy-start.6
  256.6 9.3 %copy-start.4 = (bf16[2048,384]{1,0:T(8,128)(2,1)S(1)}, bf16[2048,384]{1,0:T(8,128)(2,1)}, u32[]{:S(2)}) copy-start(bf16[2048,384]{1,0:T(8,128)(2,1)} %copy-done.3) | copy-start | bytes 4718596
  256.6 18.7 %slice-start = ((s8[8388608]{0:T(1024)(128)(4,1)}), s8[4194304]{0:T(1024)(128)(4,1)S(1)}, s32[]{:S(2)}) async-start(s8[8388608]{0:T(1024)(128)(4,1)} %bitcast.37), calls=%async_computation.8 | async-start | bytes 8388608
  266.0 9.4 %slice-start.1 = ((s8[8388608]{0:T(1024)(128)(4,1)}), s8[4194304]{0:T(1024)(128)(4,1)S(1)}, s32[]{:S(2)}) async-start(s8[8388608]{0:T(1024)(128)(4,1)} %bitcast.37), calls=%async_computation.9 | async-start | bytes 8388608
  266.0 9.4 %copy-start.9 = (f32[2048,384]{1,0:T(8,128)S(1)}, f32[2048,384]{1,0:T(8,128)}, u32[]{:S(2)}) copy-start(f32[2048,384]{1,0:T(8,128)} %fusion.7) | copy-start | bytes 9437188
  266.0 9.4 %copy-start.10 = (f32[2048,384]{1,0:T(8,128)S(1)}, f32[2048,384]{1,0:T(8,128)}, u32[]{:S(2)}) copy-start(f32[2048,384]{1,0:T(8,128)} %fusion.6) | copy-start | bytes 9437188
  275.4 132.3 %copy-start.1 = (bf16[128,2048]{1,0:T(8,128)(2,1)S(1)}, bf16[128,2048]{1,0:T(8,128)(2,1)}, u32[]{:S(2)}) copy-start(bf16[128,2048]{1,0:T(8,128)(2,1)} %param.7) | copy-start | bytes 1572868
Sparse Core Ops, SparseCore 0:
  11.4 115.0 all-gather.2
  130.0 95.1 all-gather.4
  255.4 149.0 reduce-scatter.1

commit v2 on v0

v2 whole, which is shorter than its diff:
```python
import jax
import jax.numpy as jnp
from jax import lax
from jax.sharding import PartitionSpec as P


def joined(own, other):
    first = lax.axis_index("dp") == 0
    return jnp.where(first, jnp.concatenate([own, other], -1), jnp.concatenate([other, own], -1))


def swapped(part):
    return lax.ppermute(part, "dp", [(0, 1), (1, 0)])


def placed(tokens, out_grad, route_ids, route_probs, gate_store, up_store, down_store):
    tok_rows, model_width = tokens.shape
    top_count = route_ids.shape[1]
    experts = lax.axis_size("expert")
    capacity = max(2, 9 * tok_rows * top_count // (8 * experts))
    slots = experts * capacity
    width = model_width // 2
    here = lax.axis_index("dp") * width
    there = width - here
    f32, bf16 = jnp.float32, jnp.bfloat16

    chosen = route_ids[:, :, None] == jnp.arange(experts, dtype=jnp.int32)[None, None, :]
    weight = jnp.sum(jnp.where(chosen, route_probs[:, :, None], 0.0), axis=1)
    named = jnp.any(chosen, axis=1)
    earlier = jnp.arange(tok_rows)[:, None] > jnp.arange(tok_rows)[None, :]
    rank = jnp.dot(earlier.astype(bf16), named.astype(bf16), preferred_element_type=f32)
    rank = jnp.where(named, rank, -1.0)
    hit = rank.T[:, None, :] == jnp.arange(capacity, dtype=f32)[None, :, None]
    slot_prob = jnp.sum(jnp.where(hit, weight.T[:, None, :], 0.0), axis=2)
    place = hit.astype(bf16).reshape(slots, tok_rows)

    x_part = jnp.dot(
        place, lax.dynamic_slice_in_dim(tokens, here, width, 1), preferred_element_type=f32
    ).astype(bf16)
    dy_part = (
        jnp.dot(place, lax.dynamic_slice_in_dim(out_grad, here, width, 1), preferred_element_type=f32)
        * slot_prob.reshape(slots, 1)
    ).astype(bf16)

    def exchange(a):
        return lax.all_to_all(a, "expert", split_axis=0, concat_axis=0, tiled=True)

    def panel(store):
        return lax.all_to_all(store, "expert", split_axis=0, concat_axis=1, tiled=True)[0]

    x_own = exchange(x_part.reshape(experts, capacity, width)).reshape(slots, width)
    gate_panel = panel(gate_store)
    up_panel = panel(up_store)
    dy_own = exchange(dy_part.reshape(experts, capacity, width)).reshape(slots, width)
    down_panel = panel(down_store)
    rows_in = joined(x_own, swapped(x_own))
    dy_rows = joined(dy_own, swapped(dy_own))
    gate_pre = jnp.dot(rows_in, gate_panel, preferred_element_type=f32)
    up_pre = jnp.dot(rows_in, up_panel, preferred_element_type=f32)
    sig = jax.nn.sigmoid(gate_pre)
    activation = (gate_pre * sig * up_pre).astype(bf16)
    act_grad = jnp.dot(dy_rows, down_panel, preferred_element_type=f32)
    up_grad = (act_grad * gate_pre * sig).astype(bf16)
    gate_grad = (act_grad * up_pre * sig * (1.0 + gate_pre * (1.0 - sig))).astype(bf16)
    back = (((1,), (1,)), ((), ()))

    def slot_part(start):
        rows = [lax.dynamic_slice_in_dim(w, start, width, 0) for w in (gate_panel, up_panel)]
        return lax.dot_general(gate_grad, rows[0], back, preferred_element_type=f32) + lax.dot_general(
            up_grad, rows[1], back, preferred_element_type=f32
        )

    arrived = swapped(slot_part(there).astype(bf16))
    summed = (slot_part(here) + arrived.astype(f32)).astype(bf16)
    returned = exchange(summed.reshape(experts, capacity, width)).reshape(slots, width)
    share = lax.dot_general(place, returned, (((0,), (0,)), ((), ())), preferred_element_type=f32).astype(bf16)
    grad_tokens = joined(share, swapped(share))
    outer = (((0,), (0,)), ((), ()))
    grad_down = lax.dot_general(dy_rows, activation, outer, preferred_element_type=f32).astype(bf16)
    grad_gate = lax.dot_general(rows_in, gate_grad, outer, preferred_element_type=f32).astype(bf16)
    grad_up = lax.dot_general(rows_in, up_grad, outer, preferred_element_type=f32).astype(bf16)
    return (grad_gate[None], grad_up[None], grad_down[None], grad_tokens)


def solution(mesh):
    return jax.shard_map(
        placed,
        mesh=mesh,
        in_specs=(
            P("expert", None),
            P("expert", None),
            P("expert", None),
            P("expert", None),
            P(None, "expert", "dp"),
            P(None, "expert", "dp"),
            P(None, "expert", "dp"),
        ),
        out_specs=(
            P("expert", None, "dp"),
            P("expert", None, "dp"),
            P("expert", None, "dp"),
            P("expert", None),
        ),
        check_vma=False,
    )
```

time: 371 us -> 330 us (0.89)
  blocking collectives: 2.18 us -> 46.1 us
  local copies, waits for them, and re-layouts: 39.7 us -> 0.73 us
  other arithmetic: 29.2 us -> 1.54 us
  matrix products: 42.7 us -> 59.6 us
  between operations: 14.1 us -> 0.9 us
  starting transfers between devices: 51.8 us -> 40.8 us
  waiting for transfers between devices: 185 us -> 174 us
    all_to_all x0 -> x1, blocking collectives: none -> 46.1 us  [panel(): lax.all_to_all(store, 'expert', split_axis=0, concat_axis=1, tiled=True)[0]]
    gather x6 -> x0, local copies, waits for them, and re-layouts: 27 us -> none  [the longest x1 5.94 us: on_device(): tokens[owner_row]]
    reduce_scatter x1 -> x0, waiting for transfers between devices: 18.8 us -> none  [on_device(): lax.psum_scatter(slot_half.reshape(experts, capacity, model_width), 'dp',...]
    dot_general x8 -> x14, matrix products: 42.7 us -> 59.6 us  [the longest x1 8.13 us: placed(): lax.dot_general(rows_in, up_grad, outer, preferred_element_type=f32)]
    all_to_all x6 -> x5, starting transfers between devices: 51.5 us -> 40.5 us  [the longest x3 25.6 us: exchange(): return lax.all_to_all(a, 'expert', split_axis=0, concat_axis=0, tiled=True)]
    scatter x2 -> x0, local copies, waits for them, and re-layouts: 8.63 us -> none  [the longest x1 4.32 us: on_device(): source = jnp.full((experts * capacity,), slot_total, jnp.int32).at[slot_p...]
    convert_element_type x2 -> x0, other arithmetic: 7.69 us -> none  [the longest x1 4.12 us: on_device(): summed.astype(jnp.bfloat16)]
    all_to_all x6 -> x5, waiting for transfers between devices: 165 us -> 171 us  [the longest x3 122 us: exchange(): return lax.all_to_all(a, 'expert', split_axis=0, concat_axis=0, tiled=True)]
  transfers between devices with their start and end apart: 9 -> 9, of which waited for: 6 -> 6; matrix products, arithmetic and copies ran while one was open for 22% -> 14% of each run, Pallas kernels for 0% -> 0%
where the time goes in v2:
time: 330 us; the launch traced here: 324 us
  waiting for transfers between devices  174 us (53%)
  matrix products  59.6 us (18%)
  blocking collectives  46.1 us (14%)
  starting transfers between devices  40.8 us (12%)
    all_to_all x3, waiting for transfers between devices, exchange(): return lax.all_to_all(a, 'expert', split_axis=0, concat_axis=0, tiled=True)  122 us
    all_to_all x2, waiting for transfers between devices, panel(): lax.all_to_all(store, 'expert', split_axis=0, concat_axis=1, tiled=True)[0]  48.6 us
    all_to_all x1, blocking collectives, panel(): lax.all_to_all(store, 'expert', split_axis=0, concat_axis=1, tiled=True)[0]  46.1 us
    all_to_all x3, starting transfers between devices, exchange(): return lax.all_to_all(a, 'expert', split_axis=0, concat_axis=0, tiled=True)  25.6 us
    all_to_all x2, starting transfers between devices, panel(): lax.all_to_all(store, 'expert', split_axis=0, concat_axis=1, tiled=True)[0]  14.9 us
    dot_general x1, matrix products, placed(): lax.dot_general(rows_in, up_grad, outer, preferred_element_type=f32)  8.13 us
    dot_general x1, matrix products, placed(): gate_pre = jnp.dot(rows_in, gate_panel, preferred_element_type=f32)  8.11 us
    dot_general x1, matrix products, placed(): lax.dot_general(dy_rows, activation, outer, preferred_element_type=f32)  8.06 us
  transfers between devices with their start and end apart: 9, of which 6 were waited for; matrix products, arithmetic and copies ran while one was open for 14% of the time, Pallas kernels for 0%

profile of v2, /device:TPU:0, one launch (start us, length us, event | category | flops | bytes accessed | tf_op | source)
XLA Modules:
  0.0 323.6 jit_solution(13981634180581247777)
XLA Ops:
  0.6 0.0 copy-start
  0.6 46.1 %all_to_all.42 = bf16[16,128,384]{2,1,0:T(8,128)(2,1)} all-to-all(bf16[16,128,384]{2,1,0:T(8,128)(2,1)} %param.11), channel_id=1, replica_groups=mesh['dp'=2,'expert'=16] {'expert'}, dimensions={0} | all-to-all | bytes 3145728 | tf_op jit(solution)/shard_map/all_to_all | solution.py:49
  46.8 4.1 %all-to-all-start.3 = ((bf16[16,128,384]{2,1,0:T(8,128)(2,1)}), bf16[16,128,384]{2,1,0:T(8,128)(2,1)S(1)}, u32[]{:S(2)}, u32[]{:S(2)}) async-start(bf16[16,128,384]{2,1,0:T(8,128)(2,1)} %param.12), calls=%async_computation.3 | async-start | bytes 3145728 | tf_op jit(solution)/shard_map/all_to_all | solution.py:49
  50.9 0.1 eq.49
  51.0 0.0 copy-done.6
  51.0 0.1 convolution_select_fusion
  51.1 0.2 bitcast_compare_fusion
  51.4 0.0 copy-done
  51.4 2.2 convolution_convert_fusion
  53.6 30.9 %all-to-all-done.3 = bf16[16,128,384]{2,1,0:T(8,128)(2,1)S(1)} async-done(((bf16[16,128,384]{2,1,0:T(8,128)(2,1)}), bf16[16,128,384]{2,1,0:T(8,128)(2,1)S(1)}, u32[]{:S(2)}, u32[]{:S(2)}) %all-to-all-start.3) | async-done | bytes 1572896 | tf_op jit(solution)/shard_map/all_to_all | solution.py:49
  84.5 7.5 %all-to-all-start = ((bf16[16,72,1024]{2,1,0:T(8,128)(2,1)}), bf16[16,72,1024]{2,1,0:T(8,128)(2,1)}, u32[]{:S(2)}, u32[]{:S(2)}) async-start(bf16[16,72,1024]{2,1,0:T(8,128)(2,1)} %bitcast.2), calls=%async_computation | async-start | bytes 4718592 | tf_op jit(solution)/shard_map/all_to_all | solution.py:46
  92.0 0.0 copy-done.7
  92.1 0.3 select_reduce_fusion
  92.4 0.1 mul.38
  92.5 2.3 fusion
  94.8 44.2 %all-to-all-done = bf16[16,72,1024]{2,1,0:T(8,128)(2,1)} async-done(((bf16[16,72,1024]{2,1,0:T(8,128)(2,1)}), bf16[16,72,1024]{2,1,0:T(8,128)(2,1)}, u32[]{:S(2)}, u32[]{:S(2)}) %all-to-all-start) | async-done | bytes 2359328 | tf_op jit(solution)/shard_map/all_to_all | solution.py:46
  139.0 10.8 %all-to-all-start.1 = ((bf16[16,72,1024]{2,1,0:T(8,128)(2,1)}), bf16[16,72,1024]{2,1,0:T(8,128)(2,1)}, u32[]{:S(2)}, u32[]{:S(2)}) async-start(bf16[16,72,1024]{2,1,0:T(8,128)(2,1)} %bitcast.5), calls=%async_computation.1 | async-start | bytes 4718592 | tf_op jit(solution)/shard_map/all_to_all | solution.py:46
  149.8 0.1 collective-permute-start
  149.9 46.7 %all-to-all-done.1 = bf16[16,72,1024]{2,1,0:T(8,128)(2,1)} async-done(((bf16[16,72,1024]{2,1,0:T(8,128)(2,1)}), bf16[16,72,1024]{2,1,0:T(8,128)(2,1)}, u32[]{:S(2)}, u32[]{:S(2)}) %all-to-all-start.1) | async-done | bytes 2359328 | tf_op jit(solution)/shard_map/all_to_all | solution.py:46
  196.6 10.8 %all-to-all-start.2 = ((bf16[16,128,384]{2,1,0:T(8,128)(2,1)}), bf16[16,128,384]{2,1,0:T(8,128)(2,1)}, u32[]{:S(2)}, u32[]{:S(2)}) async-start(bf16[16,128,384]{2,1,0:T(8,128)(2,1)} %param.13), calls=%async_computation.2 | async-start | bytes 3145728 | tf_op jit(solution)/shard_map/all_to_all | solution.py:49
  207.4 0.1 collective-permute-start.1
  207.5 0.0 collective-permute-done
  207.5 8.1 %fusion.29 = f32[1152,384]{1,0:T(8,128)} fusion(bf16[2048,384]{1,0:T(8,128)(2,1)} %bitcast.40, bf16[1152,1024]{1,0:T(8,128)(2,1)} %collective-permute-done, bf16[1152,1024]{1,0:T(8,128)(2,1)} %bitcast.3, pred[]{:T(512)S(6)} %eq.42), kind=kOutput, calls=%fused_computation.50 | convolution fusion | flops 1833172992 | bytes 8060929 | tf_op jit(solution)/shard_map/dot_general | solution.py:58
  215.6 7.6 %fusion.30 = f32[1152,384]{1,0:T(8,128)} fusion(bf16[2048,384]{1,0:T(8,128)(2,1)S(1)} %bitcast.37, bf16[1152,1024]{1,0:T(8,128)(2,1)} %collective-permute-done, bf16[1152,1024]{1,0:T(8,128)(2,1)} %bitcast.3, pred[]{:T(512)S(6)} %eq.42), kind=kOutput, calls=%fused_computation.51 | convolution fusion | flops 1833172992 | bytes 8060929 | tf_op jit(solution)/shard_map/dot_general | solution.py:59
  223.2 17.7 %all-to-all-done.2 = bf16[16,128,384]{2,1,0:T(8,128)(2,1)} async-done(((bf16[16,128,384]{2,1,0:T(8,128)(2,1)}), bf16[16,128,384]{2,1,0:T(8,128)(2,1)}, u32[]{:S(2)}, u32[]{:S(2)}) %all-to-all-start.2) | async-done | bytes 1572896 | tf_op jit(solution)/shard_map/all_to_all | solution.py:49
  240.9 0.0 collective-permute-done.1
  240.9 7.5 %multiply_convert_fusion.1 = (bf16[1152,384]{1,0:T(8,128)(2,1)S(1)}, bf16[1152,384]{1,0:T(8,128)(2,1)S(1)}) fusion(f32[1152,384]{1,0:T(8,128)} %fusion.29, f32[1152,384]{1,0:T(8,128)} %fusion.30, bf16[2048,384]{1,0:T(8,128)(2,1)} %bitcast.7, bf16[1152,1024]{1,0:T(8,128)(2,1)} %collective-permute-done.1, bf16[1152,1024]{1,0:T(8,128)(2,1)} %bitcast.6, ...), kind=kOutput, calls=%fused_computation.16 | convolution fusion | flops 1838923776 | bytes 11599873 | tf_op jit(solution)/shard_map/dot_general | solution.py:62
  248.4 0.0 copy-start.1
  248.4 0.0 copy-start.4
  248.4 1.4 fusion.9
  249.9 1.5 fusion.1
  251.3 0.1 collective-permute-start.2
  251.4 1.4 fusion.14
  252.9 3.1 collective-permute-done.2
  255.9 2.9 add_convert_fusion
  258.9 7.3 %all-to-all-start.5 = ((bf16[16,72,1024]{2,1,0:T(8,128)(2,1)}), bf16[16,72,1024]{2,1,0:T(8,128)(2,1)S(1)}, u32[]{:S(2)}, u32[]{:S(2)}) async-start(bf16[16,72,1024]{2,1,0:T(8,128)(2,1)} %bitcast.36), calls=%async_computation.5 | async-start | bytes 4718592 | tf_op jit(solution)/shard_map/all_to_all | solution.py:46
  266.1 0.0 copy-start.8
  266.2 0.0 copy-start.9
  266.2 8.1 %fusion.3 = bf16[1,2048,384]{2,1,0:T(8,128)(2,1)} fusion(bf16[1152,384]{1,0:T(8,128)(2,1)} %copy-done.4, bf16[1152,1024]{1,0:T(8,128)(2,1)} %collective-permute-done, bf16[1152,1024]{1,0:T(8,128)(2,1)} %bitcast.3, pred[]{:T(512)S(6)} %eq.42), kind=kOutput, calls=%fused_computation.13 | convolution fusion | flops 1833959424 | bytes 7176193 | tf_op jit(solution)/shard_map/dot_general | solution.py:81
  274.3 0.0 copy-done.9
  274.3 8.1 %fusion.4 = bf16[1,2048,384]{2,1,0:T(8,128)(2,1)} fusion(f32[1152,384]{1,0:T(8,128)S(1)} %copy-done.9, f32[1152,384]{1,0:T(8,128)S(1)} %copy-done.8, bf16[1152,1024]{1,0:T(8,128)(2,1)} %collective-permute-done.1, bf16[1152,1024]{1,0:T(8,128)(2,1)} %bitcast.6, pred[]{:T(512)S(6)} %eq.42), kind=kOutput, calls=%fused_computation.14 | convolution fusion | flops 1836613632 | bytes 9830401 | tf_op jit(solution)/shard_map/dot_general | solution.py:79
  282.4 31.3 %all-to-all-done.5 = bf16[16,72,1024]{2,1,0:T(8,128)(2,1)S(1)} async-done(((bf16[16,72,1024]{2,1,0:T(8,128)(2,1)}), bf16[16,72,1024]{2,1,0:T(8,128)(2,1)S(1)}, u32[]{:S(2)}, u32[]{:S(2)}) %all-to-all-start.5) | async-done | bytes 2359328 | tf_op jit(solution)/shard_map/all_to_all | solution.py:46
  313.7 0.6 fusion.5
  314.3 0.1 collective-permute-start.3
  314.3 0.5 copy-done.2
  314.9 7.8 %fusion.2 = bf16[1,2048,384]{2,1,0:T(8,128)(2,1)} fusion(bf16[1152,384]{1,0:T(8,128)(2,1)S(1)} %copy-done.2, bf16[1152,1024]{1,0:T(8,128)(2,1)} %collective-permute-done, bf16[1152,1024]{1,0:T(8,128)(2,1)} %bitcast.3, pred[]{:T(512)S(6)} %eq.42), kind=kOutput, calls=%fused_computation.12 | convolution fusion | flops 1833959424 | bytes 7176193 | tf_op jit(solution)/shard_map/dot_general | solution.py:80
  322.7 0.0 collective-permute-done.3
  322.7 0.9 maximum_select_fusion.4
  (13 shorter events, 0.1 us)
Async XLA Ops:
  0.6 50.8 %copy-start = (bf16[128,2048]{1,0:T(8,128)(2,1)S(1)}, bf16[128,2048]{1,0:T(8,128)(2,1)}, u32[]{:S(2)}) copy-start(bf16[128,2048]{1,0:T(8,128)(2,1)} %param.7) | copy-start | bytes 1572868
  46.8 4.2 %copy-start.6 = (s32[128,8]{0,1:T(8,128)S(1)}, s32[128,8]{0,1:T(8,128)}, u32[]{:S(2)}) copy-start(s32[128,8]{0,1:T(8,128)} %param.9) | copy-start | bytes 12292
  46.8 37.7 %all-to-all-start.3 = ((bf16[16,128,384]{2,1,0:T(8,128)(2,1)}), bf16[16,128,384]{2,1,0:T(8,128)(2,1)S(1)}, u32[]{:S(2)}, u32[]{:S(2)}) async-start(bf16[16,128,384]{2,1,0:T(8,128)(2,1)} %param.12), calls=%async_computation.3 | async-start | bytes 3145728 | tf_op jit(solution)/shard_map/all_to_all | solution.py:49
  84.5 7.6 %copy-start.7 = (f32[128,8]{0,1:T(8,128)S(1)}, f32[128,8]{0,1:T(8,128)}, u32[]{:S(2)}) copy-start(f32[128,8]{0,1:T(8,128)} %param.10) | copy-start | bytes 12292
  84.5 8.0 %copy-start.5 = (bf16[128,2048]{1,0:T(8,128)(2,1)S(1)}, bf16[128,2048]{1,0:T(8,128)(2,1)}, u32[]{:S(2)}) copy-start(bf16[128,2048]{1,0:T(8,128)(2,1)} %param.8) | copy-start | bytes 1572868
  84.5 54.5 %all-to-all-start = ((bf16[16,72,1024]{2,1,0:T(8,128)(2,1)}), bf16[16,72,1024]{2,1,0:T(8,128)(2,1)}, u32[]{:S(2)}, u32[]{:S(2)}) async-start(bf16[16,72,1024]{2,1,0:T(8,128)(2,1)} %bitcast.2), calls=%async_computation | async-start | bytes 4718592 | tf_op jit(solution)/shard_map/all_to_all | solution.py:46
  139.0 57.6 %all-to-all-start.1 = ((bf16[16,72,1024]{2,1,0:T(8,128)(2,1)}), bf16[16,72,1024]{2,1,0:T(8,128)(2,1)}, u32[]{:S(2)}, u32[]{:S(2)}) async-start(bf16[16,72,1024]{2,1,0:T(8,128)(2,1)} %bitcast.5), calls=%async_computation.1 | async-start | bytes 4718592 | tf_op jit(solution)/shard_map/all_to_all | solution.py:46
  149.8 57.6 %collective-permute-start = (bf16[1152,1024]{1,0:T(8,128)(2,1)}, bf16[1152,1024]{1,0:T(8,128)(2,1)}, u32[]{:S(2)}, u32[]{:S(2)}) collective-permute-start(bf16[1152,1024]{1,0:T(8,128)(2,1)} %bitcast.3), channel_id=1, source_target_pairs={{0,16},{16,0},{1,17},{17,1},{2,18},{18,2},{3,19},{19,3},{4,20},{20... | collective-permute-start | bytes 7077896 | tf_op jit(solution)/shard_map/ppermute | solution.py:13
  196.6 44.3 %all-to-all-start.2 = ((bf16[16,128,384]{2,1,0:T(8,128)(2,1)}), bf16[16,128,384]{2,1,0:T(8,128)(2,1)}, u32[]{:S(2)}, u32[]{:S(2)}) async-start(bf16[16,128,384]{2,1,0:T(8,128)(2,1)} %param.13), calls=%async_computation.2 | async-start | bytes 3145728 | tf_op jit(solution)/shard_map/all_to_all | solution.py:49
  207.4 33.5 %collective-permute-start.1 = (bf16[1152,1024]{1,0:T(8,128)(2,1)}, bf16[1152,1024]{1,0:T(8,128)(2,1)}, u32[]{:S(2)}, u32[]{:S(2)}) collective-permute-start(bf16[1152,1024]{1,0:T(8,128)(2,1)} %bitcast.6), channel_id=1, source_target_pairs={{0,16},{16,0},{1,17},{17,1},{2,18},{18,2},{3,19},{19,3},{4,20},{20... | collective-permute-start | bytes 7077896 | tf_op jit(solution)/shard_map/ppermute | solution.py:13
  240.9 7.5 %copy-start.3 = (bf16[16,128,384]{2,1,0:T(8,128)(2,1)S(1)}, bf16[16,128,384]{2,1,0:T(8,128)(2,1)}, u32[]{:S(2)}) copy-start(bf16[16,128,384]{2,1,0:T(8,128)(2,1)} %all_to_all.42) | copy-start | bytes 4718596
  248.4 3.0 copy-start.1
  248.4 7.5 %copy-start.4 = (bf16[1152,384]{1,0:T(8,128)(2,1)}, bf16[1152,384]{1,0:T(8,128)(2,1)S(1)}, u32[]{:S(2)}) copy-start(bf16[1152,384]{1,0:T(8,128)(2,1)S(1)} %get-tuple-element.4) | copy-start | bytes 2654212
  251.3 4.6 %collective-permute-start.2 = (bf16[1152,1024]{1,0:T(8,128)(2,1)S(1)}, bf16[1152,1024]{1,0:T(8,128)(2,1)S(1)}, u32[]{:S(2)}, u32[]{:S(2)}) collective-permute-start(bf16[1152,1024]{1,0:T(8,128)(2,1)S(1)} %fusion.1), channel_id=1, source_target_pairs={{0,16},{16,0},{1,17},{17,1},{2,18},{18,2},{3,19},{19,3},{4,20},{20... | collective-permute-start | bytes 7077896 | tf_op jit(solution)/shard_map/ppermute | solution.py:13
  258.9 54.8 %all-to-all-start.5 = ((bf16[16,72,1024]{2,1,0:T(8,128)(2,1)}), bf16[16,72,1024]{2,1,0:T(8,128)(2,1)S(1)}, u32[]{:S(2)}, u32[]{:S(2)}) async-start(bf16[16,72,1024]{2,1,0:T(8,128)(2,1)} %bitcast.36), calls=%async_computation.5 | async-start | bytes 4718592 | tf_op jit(solution)/shard_map/all_to_all | solution.py:46
  266.1 8.2 %copy-start.8 = (f32[1152,384]{1,0:T(8,128)S(1)}, f32[1152,384]{1,0:T(8,128)}, u32[]{:S(2)}) copy-start(f32[1152,384]{1,0:T(8,128)} %fusion.29) | copy-start | bytes 5308420
  266.2 8.1 %copy-start.9 = (f32[1152,384]{1,0:T(8,128)S(1)}, f32[1152,384]{1,0:T(8,128)}, u32[]{:S(2)}) copy-start(f32[1152,384]{1,0:T(8,128)} %fusion.30) | copy-start | bytes 5308420
  313.7 1.2 copy-start.2
  314.3 8.4 %collective-permute-start.3 = (bf16[128,1024]{1,0:T(8,128)(2,1)S(1)}, bf16[128,1024]{1,0:T(8,128)(2,1)S(1)}, u32[]{:S(2)}, u32[]{:S(2)}) collective-permute-start(bf16[128,1024]{1,0:T(8,128)(2,1)S(1)} %fusion.5), channel_id=1, source_target_pairs={{0,16},{16,0},{1,17},{17,1},{2,18},{18,2},{3,19},{19,3},{4,20},{20... | collective-permute-start | bytes 786440 | tf_op jit(solution)/shard_map/ppermute | solution.py:13
